TPU v7x, 256 devices: a whole 4x4x8 slice. The times are simulated.
256 devices in a mesh: gx: 8 (over z), gy: 4 (over y_lo, core), gz: 8 (over y_hi, x).
Axes of the slice: x: 4, y: 4 (y_hi: 2, y_lo: 2; y = y_hi * 2 + y_lo), z: 8, core: 2. Of those that a mesh axis runs over, the one named last changes fastest.
Arguments:
- state: bfloat16 [128, 64, 16, 8, 128], P('gx', 'gy', 'gz'), may hold values from -6 to 6
- cotangent: bfloat16 [128, 64, 16, 8, 128], P('gx', 'gy', 'gz'), may hold values from -6 to 6
- counts: int32 [8], P('gz'), may hold values from 1 to 2, 12 in all
- edge_weights: bfloat16 [2, 2, 128, 128], replicated, may hold values from -0.5 to 0.5
- node_in: bfloat16 [2, 256, 128], replicated, may hold values from -0.375 to 0.375
- node_out: bfloat16 [2, 128, 128], replicated, may hold values from -0.5 to 0.5
- biases: float32 [2, 2, 128], replicated, may hold values from -4 to 4
Outputs:
- state_grad: bfloat16 [128, 64, 16, 8, 128], P('gx', 'gy', 'gz')
- edge_grads: float32 [2, 2, 128, 128], replicated
- node_in_grad: float32 [2, 256, 128], replicated
- node_out_grad: float32 [2, 128, 128], replicated
- bias_grads: float32 [2, 2, 128], replicated
Inputs may be any that keep to these rules, and one draw needn't show every extreme that they name: The counts sum to 12; index k of gz holds the element layers that follow those of smaller indices.
All inputs are finite; a program needn't handle non-finite values. No bound on the sum of `counts` on one device may be relied on, other than what follows from the above.
Results may differ from a plain program's by a relative error of at most 0.012.
The roundings to bfloat16 on the way count: a program that leaves them out, or rounds other values in their place, can miss the bound.
Values sent between devices are 32-bit elements; how exact they have to be, the bound alone decides.
A program may use at most 128 MiB of HBM per device.

v0:
```python
import math
import jax
import jax.numpy as jnp
from jax import lax
from jax.sharding import PartitionSpec as P

edge_dims = (1, 3, 5)


def with_halo(cells, sides, width):
    for axis, dim in sides:
        count = lax.axis_size(axis)
        ends = count - 1
        head = lax.slice_in_dim(cells, 0, width, axis=dim)
        tail = lax.slice_in_dim(cells, cells.shape[dim] - width, cells.shape[dim], axis=dim)
        cells = jnp.concatenate(
            [
                lax.ppermute(tail, axis, [(i, (i + 1) % count) for i in range(ends)]),
                cells,
                lax.ppermute(head, axis, [((i + 1) % count, i) for i in range(ends)]),
            ],
            axis=dim,
        )
    return cells


def slice_along(array, start, stop, dim_no):
    return lax.slice_in_dim(array, start, stop, axis=dim_no)


def matmul_rows(left, weight):
    flattened = left.reshape(-1, left.shape[-1])
    product = jnp.dot(flattened, weight, preferred_element_type=jnp.float32)
    return product.reshape(left.shape[:-1] + (weight.shape[-1],))


def cross_rows(left, right):
    return lax.dot_general(
        left.reshape(-1, left.shape[-1]),
        right.reshape(-1, right.shape[-1]),
        (((0,), (0,)), ((), ())),
        preferred_element_type=jnp.float32,
    )


def spread_diff(values, dim_no):
    zero_row = jnp.zeros_like(slice_along(values, 0, 1, dim_no))
    return jnp.concatenate([zero_row, values], dim_no) - jnp.concatenate([values, zero_row], dim_no)


def silu_slope(values):
    sig_value = jax.nn.sigmoid(values)
    return sig_value * (1.0 + values * (1.0 - sig_value))


def edges_forward(features, weight_one, weight_two, bias_edge):
    widened = features.astype(jnp.float32)
    messages = jnp.zeros(features.shape, jnp.float32)
    stored = []
    for dim_no in edge_dims:
        length = features.shape[dim_no]
        differ = (
            slice_along(widened, 1, length, dim_no) - slice_along(widened, 0, length - 1, dim_no)
        ).astype(jnp.bfloat16)
        before = matmul_rows(differ, weight_one) + bias_edge
        active = jax.nn.silu(before).astype(jnp.bfloat16)
        messages = messages + spread_diff(matmul_rows(active, weight_two), dim_no)
        stored.append((differ, before, active))
    return (messages, stored)


def edges_backward(grad_msg, stored, weight_one, weight_two):
    feat_width = grad_msg.shape[-1]
    grad_feat = jnp.zeros(grad_msg.shape, jnp.float32)
    grad_one = jnp.zeros((feat_width, feat_width), jnp.float32)
    grad_two = jnp.zeros((feat_width, feat_width), jnp.float32)
    grad_bias = jnp.zeros((feat_width,), jnp.float32)
    for dim_no, entry in zip(edge_dims, stored):
        differ, before, active = entry
        length = grad_msg.shape[dim_no]
        grad_out = (
            slice_along(grad_msg, 1, length, dim_no) - slice_along(grad_msg, 0, length - 1, dim_no)
        ).astype(jnp.bfloat16)
        grad_two = grad_two + cross_rows(active, grad_out)
        grad_pre = (matmul_rows(grad_out, weight_two.T) * silu_slope(before)).astype(jnp.bfloat16)
        grad_one = grad_one + cross_rows(differ, grad_pre)
        grad_bias = grad_bias + jnp.sum(grad_pre.astype(jnp.float32).reshape(-1, feat_width), 0)
        grad_feat = grad_feat + spread_diff(matmul_rows(grad_pre, weight_one.T), dim_no)
    return (grad_feat, grad_one, grad_two, grad_bias)


def node_forward(features, summed, weight_in, weight_out, bias_node):
    joined = jnp.concatenate([features, summed.astype(jnp.bfloat16)], -1)
    before = matmul_rows(joined, weight_in) + bias_node
    active = jax.nn.silu(before).astype(jnp.bfloat16)
    result = (features.astype(jnp.float32) + matmul_rows(active, weight_out)).astype(jnp.bfloat16)
    return (result, (joined, before, active))


def node_backward(grad_next, stored, weight_in, weight_out):
    joined, before, active = stored
    feat_width = grad_next.shape[-1]
    grad_out_w = cross_rows(active, grad_next)
    grad_pre = (matmul_rows(grad_next, weight_out.T) * silu_slope(before)).astype(jnp.bfloat16)
    grad_in_w = cross_rows(joined, grad_pre)
    grad_bias = jnp.sum(grad_pre.astype(jnp.float32).reshape(-1, feat_width), 0)
    grad_joined = matmul_rows(grad_pre, weight_in.T)
    grad_feat = grad_next.astype(jnp.float32) + grad_joined[..., :feat_width]
    return (grad_feat, grad_joined[..., feat_width:], grad_in_w, grad_out_w, grad_bias)


def couple(array, elem_dim, node_dim):
    moved = jnp.moveaxis(array, (elem_dim, node_dim), (0, 1))
    front_face = moved[:, 0]
    back_face = moved[:, -1]
    zero_face = jnp.zeros_like(front_face[:1])
    new_front = front_face + jnp.concatenate([zero_face, back_face[:-1]], 0)
    new_back = back_face + jnp.concatenate([front_face[1:], zero_face], 0)
    joined = jnp.concatenate([new_front[:, None], moved[:, 1:-1], new_back[:, None]], 1)
    return jnp.moveaxis(joined, (0, 1), (elem_dim, node_dim))


def local_couple(values, dim_no, nodes_edge):
    full_shape = values.shape
    elems_here = full_shape[dim_no] // nodes_edge
    split_shape = full_shape[:dim_no] + (elems_here, nodes_edge) + full_shape[dim_no + 1 :]
    return couple(values.reshape(split_shape), dim_no, dim_no + 1).reshape(full_shape)


def fold_rim(extended, dim_no):
    inner_len = extended.shape[dim_no] - 2
    core_rows = slice_along(extended, 1, inner_len + 1, dim_no)
    front_row = slice_along(core_rows, 0, 1, dim_no) + slice_along(extended, 0, 1, dim_no)
    back_row = slice_along(core_rows, inner_len - 1, inner_len, dim_no) + slice_along(
        extended, inner_len + 1, inner_len + 2, dim_no
    )
    return jnp.concatenate(
        [front_row, slice_along(core_rows, 1, inner_len - 1, dim_no), back_row], dim_no
    )


def on_device(state, cotangent, counts, edge_weights, node_in, node_out, biases):
    nodes_edge = state.shape[3]
    span_x = state.shape[0]
    span_y = state.shape[1]
    elems_x = span_x // nodes_edge
    elems_y = span_y // nodes_edge
    slot_count = state.shape[2]
    grid_shape = state.shape[:4]
    filled = counts[0]
    slot_ids = jnp.arange(slot_count, dtype=jnp.int32)
    node_ids = jnp.arange(nodes_edge, dtype=jnp.int32)
    live_mask = (slot_ids < filled).astype(jnp.float32)[None, None, :, None, None]

    def edge_mult(position, axis_len, elems_here):
        place = jnp.arange(elems_here * nodes_edge, dtype=jnp.int32)
        node_here = place % nodes_edge
        elem_global = position * elems_here + place // nodes_edge
        front_pair = ((node_here == 0) & (elem_global > 0)).astype(jnp.float32)
        back_pair = (
            (node_here == nodes_edge - 1) & (elem_global < elems_here * axis_len - 1)
        ).astype(jnp.float32)
        return 1.0 + front_pair + back_pair

    mult_x = edge_mult(lax.axis_index("gx"), lax.axis_size("gx"), elems_x)
    mult_y = edge_mult(lax.axis_index("gy"), lax.axis_size("gy"), elems_y)
    index_z = lax.axis_index("gz")
    size_z = lax.axis_size("gz")
    lower_mult = ((slot_ids > 0) | (index_z > 0)).astype(jnp.float32)
    upper_mult = ((slot_ids < filled - 1) | (index_z < size_z - 1)).astype(jnp.float32)
    mult_z = (
        1.0
        + (node_ids == 0).astype(jnp.float32)[None, :] * lower_mult[:, None]
        + (node_ids == nodes_edge - 1).astype(jnp.float32)[None, :] * upper_mult[:, None]
    )
    copies = (
        mult_x[:, None, None, None, None]
        * mult_y[None, :, None, None, None]
        * mult_z[None, None, :, :, None]
    )

    def couple_all(values):
        inner = local_couple(local_couple(values, 0, nodes_edge), 1, nodes_edge)
        extended = with_halo(inner, (("gx", 0), ("gy", 1)), 1)
        coupled = fold_rim(fold_rim(extended, 0), 1)
        top_faces = coupled[:, :, :, -1]
        bottom_faces = coupled[:, :, :, 0]
        top_used = lax.dynamic_index_in_dim(top_faces, filled - 1, 2, keepdims=False)
        rim_pair = jnp.stack([bottom_faces[:, :, 0], top_used], 2)
        rim_ext = with_halo(rim_pair, (("gz", 2),), 1)
        from_below = rim_ext[:, :, 0]
        from_above = rim_ext[:, :, 3]
        below_add = jnp.concatenate([from_below[:, :, None], top_faces[:, :, :-1]], 2)
        last_slot = (slot_ids == filled - 1).astype(jnp.float32)[None, None, :, None]
        above_add = (
            jnp.concatenate([bottom_faces[:, :, 1:], jnp.zeros_like(bottom_faces[:, :, :1])], 2)
            + last_slot * from_above[:, :, None]
        )
        result = jnp.concatenate(
            [
                (bottom_faces + below_add)[:, :, :, None],
                coupled[:, :, :, 1:-1],
                (top_faces + above_add)[:, :, :, None],
            ],
            3,
        )
        return result * live_mask

    def to_cells(array):
        return array.reshape(
            (elems_x, nodes_edge, elems_y, nodes_edge, slot_count, nodes_edge, array.shape[-1])
        )

    def to_grid(array):
        return array.reshape(grid_shape + (array.shape[-1],))

    features = state
    grad_next = cotangent * live_mask.astype(jnp.bfloat16)
    saved = []
    for layer_no in range(2):
        messages, edge_store = edges_forward(
            to_cells(features),
            edge_weights[layer_no, 0],
            edge_weights[layer_no, 1],
            biases[layer_no, 0],
        )
        summed = couple_all(to_grid(messages) * live_mask) / copies
        result, node_store = node_forward(
            features, summed, node_in[layer_no], node_out[layer_no], biases[layer_no, 1]
        )
        saved.append((edge_store, node_store))
        features = result
    per_layer = [None, None]
    for layer_no in (1, 0):
        edge_store, node_store = saved[layer_no]
        grad_feat, grad_sum, grad_in_w, grad_out_w, grad_node_b = node_backward(
            grad_next, node_store, node_in[layer_no], node_out[layer_no]
        )
        grad_msg = couple_all(grad_sum / copies * live_mask)
        grad_edge, grad_one, grad_two, grad_edge_b = edges_backward(
            to_cells(grad_msg), edge_store, edge_weights[layer_no, 0], edge_weights[layer_no, 1]
        )
        grad_next = (grad_feat + to_grid(grad_edge)).astype(jnp.bfloat16)
        local_terms = (
            jnp.stack([grad_one, grad_two]),
            grad_in_w,
            grad_out_w,
            jnp.stack([grad_edge_b, grad_node_b]),
        )
        per_layer[layer_no] = local_terms
    stacked = tuple(
        (jnp.stack([per_layer[0][pos_no], per_layer[1][pos_no]]) for pos_no in range(4))
    )
    stacked = lax.psum(stacked, ("gx", "gy", "gz"))
    layers_all = 3 * slot_count * size_z // 4
    nodes_all = (
        nodes_edge**3 * elems_x * lax.axis_size("gx") * elems_y * lax.axis_size("gy") * layers_all
    )
    grad_scale = 1.0 / math.sqrt(nodes_all)
    state_grad = grad_next * live_mask.astype(jnp.bfloat16)
    return (
        state_grad,
        stacked[0] * grad_scale,
        stacked[1] * grad_scale,
        stacked[2] * grad_scale,
        stacked[3] * grad_scale,
    )


def solution(mesh):
    return jax.shard_map(
        on_device,
        mesh=mesh,
        in_specs=(
            P("gx", "gy", "gz", None, None),
            P("gx", "gy", "gz", None, None),
            P("gz"),
            P(),
            P(),
            P(),
            P(),
        ),
        out_specs=(P("gx", "gy", "gz", None, None), P(), P(), P(), P()),
        check_vma=False,
    )
```

profile of v0, /device:TPU:1, one launch (start us, length us, event | category | flops | bytes accessed | tf_op | source)
XLA Modules:
  0.0 601.1 jit_solution(5968325419626531154)
XLA Ops:
  27.5 4.4 collective-permute-start
  33.2 2.4 copy_bitcast_fusion.7
  35.6 2.9 collective-permute-done.1
  40.3 4.7 collective-permute-start.2
  45.0 2.1 collective-permute-start.3
  47.4 4.4 collective-permute-done.3
  56.4 3.1 collective-permute-start.4
  63.2 4.5 collective-permute-done.5
  70.3 2.1 multiply_convert_fusion.3
  88.6 3.6 collective-permute-start.6
  94.8 5.2 collective-permute-done.7
  100.2 4.2 collective-permute-start.8
  106.5 4.4 collective-permute-done.9
  112.7 3.6 collective-permute-start.10
  121.6 3.5 collective-permute-done.11
  133.8 4.6 collective-permute-start.12
  140.9 4.1 collective-permute-done.13
  145.3 4.2 collective-permute-start.14
  149.5 1.9 collective-permute-start.15
  152.4 3.6 collective-permute-done.15
  157.7 5.7 collective-permute-start.16
  168.5 3.4 collective-permute-done.17
  192.4 3.6 collective-permute-start.18
  199.0 3.5 collective-permute-done.19
  202.7 4.2 collective-permute-start.20
  209.5 3.8 collective-permute-done.21
  215.2 7.3 %collective-permute-start.22 = (f32[16,16,1,128]{3,1,0,2:T(8,128)S(1)}, f32[16,16,1,128]{3,1,0,2:T(8,128)S(1)}, u32[]{:S(2)}, u32[]{:S(2)}) collective-permute-start(f32[16,16,1,128]{3,1,0,2:T(8,128)S(1)} %dynamic-slice_bitcast_fusion), channel_id=1, source_target_pairs={{0,1},{1,2},{2,3},{3,4},{4,5},{5,6},{6,7},{8,9},{9,10},{10,11},{11... | collective-permute-start | bytes 393224 | tf_op jit(solution)/shard_map/ppermute | solution.py:18
  227.5 3.4 collective-permute-done.23
  246.3 84.3 %psum.31 = f32[2,2,128]{2,1,0:T(2,128)S(1)} all-reduce(f32[2,2,128]{2,1,0:T(2,128)S(1)} %pad_maximum_fusion.51), channel_id=1, replica_groups=mesh['gx'=8,'gy'=4,'gz'=8] {'gx','gy','gz'}, use_global_device_ids=true, to_apply=%region_11.12 | all-reduce | flops 512 | bytes 4096 | tf_op jit(solution)/shard_map/psum | solution.py:254
  331.2 2.8 fusion.131
  336.7 4.3 subtract_add_fusion
  342.6 246.3 %all-reduce.47.cloned.1.call-done = (f32[2,2,128,128]{3,2,1,0:T(8,128)}, f32[2,256,128]{2,1,0:T(8,128)}, f32[2,128,128]{2,1,0:T(8,128)}) async-done(((f32[2,2,128,128]{3,2,1,0:T(8,128)}, f32[2,256,128]{2,1,0:T(8,128)}, f32[2,128,128]{2,1,0:T(8,128)}), (f32[2,2,128,128]{3,2,1,0:T(8,128)}, f32[2,256,128]{2,1,0:T(8,128)}, f32[2,128,128]{2,1,0:T(8,128)})) %all-reduce.47.cloned.1.call-update) | async-done | bytes 655376 | tf_op jit(solution)/shard_map/psum | solution.py:254
  (332 shorter events, 138.0 us)
Async XLA Ops:
  7.2 581.7 %all-reduce.47.cloned.1.call-start = ((), (), s32[]{:S(2)}) async-start(), calls=%async_computation | async-start | bytes 1310720 | tf_op jit(solution)/shard_map/psum | solution.py:254
  8.9 6.6 %copy-start.14 = (bf16[2,7,2,8,2,8,128]{6,5,4,3,2,1,0:T(8,128)(2,1)}, bf16[2,7,2,8,2,8,128]{6,5,4,3,2,1,0:T(8,128)(2,1)S(1)}, u32[]{:S(2)}) copy-start(bf16[2,7,2,8,2,8,128]{6,5,4,3,2,1,0:T(8,128)(2,1)S(1)} %fusion.22) | copy-start | bytes 2752516
  12.3 7.7 %copy-start.28 = (f32[128]{0:T(128)}, f32[128]{0:T(128)S(1)}, u32[]{:S(2)}) copy-start(f32[128]{0:T(128)S(1)} %get-tuple-element.80) | copy-start | bytes 1540
  25.7 7.5 %copy-start.4 = (f32[2,16,2,8,128]{4,0,3,2,1:T(2,128)}, f32[2,16,2,8,128]{4,0,3,2,1:T(2,128)S(1)}, u32[]{:S(2)}) copy-start(f32[2,16,2,8,128]{4,0,3,2,1:T(2,128)S(1)} %copy_add_fusion.4) | copy-start | bytes 786436
  27.5 8.1 %collective-permute-start = (f32[1,16,2,8,128]{4,1,0,3,2:T(8,128)}, f32[1,16,2,8,128]{4,1,0,3,2:T(8,128)S(1)}, u32[]{:S(2)}, u32[]{:S(2)}) collective-permute-start(f32[1,16,2,8,128]{4,1,0,3,2:T(8,128)} %get-tuple-element.56), channel_id=1, source_target_pairs={{0,32},{32,64},{64,96},{96,128},{128,160},{160,192},{192,224},{1,3... | collective-permute-start | bytes 393224 | tf_op jit(solution)/shard_map/ppermute | solution.py:18
  31.8 6.7 %collective-permute-start.1 = (f32[1,16,2,8,128]{4,1,0,3,2:T(8,128)}, f32[1,16,2,8,128]{4,1,0,3,2:T(8,128)}, u32[]{:S(2)}, u32[]{:S(2)}) collective-permute-start(f32[1,16,2,8,128]{4,1,0,3,2:T(8,128)} %get-tuple-element.57), channel_id=1, source_target_pairs={{32,0},{64,32},{96,64},{128,96},{160,128},{192,160},{224,192},{33,... | collective-permute-start | bytes 393224 | tf_op jit(solution)/shard_map/ppermute | solution.py:20
  40.3 7.1 %collective-permute-start.2 = (f32[18,1,2,8,128]{4,1,0,3,2:T(1,128)}, f32[18,1,2,8,128]{4,1,0,3,2:T(1,128)S(1)}, u32[]{:S(2)}, u32[]{:S(2)}) collective-permute-start(f32[18,1,2,8,128]{4,1,0,3,2:T(1,128)} %get-tuple-element.30), channel_id=1, source_target_pairs={{0,8},{8,16},{16,24},{1,9},{9,17},{17,25},{2,10},{10,18},{18,26},{... | collective-permute-start | bytes 442376 | tf_op jit(solution)/shard_map/ppermute | solution.py:18
  45.0 6.8 %collective-permute-start.3 = (f32[18,1,2,8,128]{4,1,0,3,2:T(1,128)}, f32[18,1,2,8,128]{4,1,0,3,2:T(1,128)}, u32[]{:S(2)}, u32[]{:S(2)}) collective-permute-start(f32[18,1,2,8,128]{4,1,0,3,2:T(1,128)} %get-tuple-element.31), channel_id=1, source_target_pairs={{8,0},{16,8},{24,16},{9,1},{17,9},{25,17},{10,2},{18,10},{26,18},{... | collective-permute-start | bytes 442376 | tf_op jit(solution)/shard_map/ppermute | solution.py:20
  47.4 5.9 copy-start.5
  56.4 5.1 collective-permute-start.4
  61.6 6.1 %collective-permute-start.5 = (f32[16,16,1,128]{3,1,0,2:T(8,128)S(1)}, f32[16,16,1,128]{3,1,0,2:T(8,128)S(1)}, u32[]{:S(2)}, u32[]{:S(2)}) collective-permute-start(f32[16,16,1,128]{3,1,0,2:T(8,128)S(1)} %get-tuple-element.76), channel_id=1, source_target_pairs={{1,0},{2,1},{3,2},{4,3},{5,4},{6,5},{7,6},{9,8},{10,9},{11,10},{12... | collective-permute-start | bytes 393224 | tf_op jit(solution)/shard_map/ppermute | solution.py:20
  88.6 6.2 %collective-permute-start.6 = (f32[1,16,2,8,128]{4,1,0,2,3:T(8,128)S(1)}, f32[1,16,2,8,128]{4,1,0,2,3:T(8,128)S(1)}, u32[]{:S(2)}, u32[]{:S(2)}) collective-permute-start(f32[1,16,2,8,128]{4,1,0,2,3:T(8,128)S(1)} %get-tuple-element.48), channel_id=1, source_target_pairs={{0,32},{32,64},{64,96},{96,128},{128,160},{160,192},{192,224},{1,3... | collective-permute-start | bytes 393224 | tf_op jit(solution)/shard_map/ppermute | solution.py:18
  92.2 7.8 %collective-permute-start.7 = (f32[1,16,2,8,128]{4,1,0,2,3:T(8,128)S(1)}, f32[1,16,2,8,128]{4,1,0,2,3:T(8,128)S(1)}, u32[]{:S(2)}, u32[]{:S(2)}) collective-permute-start(f32[1,16,2,8,128]{4,1,0,2,3:T(8,128)S(1)} %get-tuple-element.49), channel_id=1, source_target_pairs={{32,0},{64,32},{96,64},{128,96},{160,128},{192,160},{224,192},{33,... | collective-permute-start | bytes 393224 | tf_op jit(solution)/shard_map/ppermute | solution.py:20
  100.2 6.3 %collective-permute-start.8 = (f32[18,1,2,8,128]{4,1,0,2,3:T(1,128)S(1)}, f32[18,1,2,8,128]{4,1,0,2,3:T(1,128)S(1)}, u32[]{:S(2)}, u32[]{:S(2)}) collective-permute-start(f32[18,1,2,8,128]{4,1,0,2,3:T(1,128)S(1)} %get-tuple-element.28), channel_id=1, source_target_pairs={{0,8},{8,16},{16,24},{1,9},{9,17},{17,25},{2,10},{10,18},{18,26},{... | collective-permute-start | bytes 442376 | tf_op jit(solution)/shard_map/ppermute | solution.py:18
  104.4 6.5 %collective-permute-start.9 = (f32[18,1,2,8,128]{4,1,0,2,3:T(1,128)S(1)}, f32[18,1,2,8,128]{4,1,0,2,3:T(1,128)S(1)}, u32[]{:S(2)}, u32[]{:S(2)}) collective-permute-start(f32[18,1,2,8,128]{4,1,0,2,3:T(1,128)S(1)} %get-tuple-element.29), channel_id=1, source_target_pairs={{8,0},{16,8},{24,16},{9,1},{17,9},{25,17},{10,2},{18,10},{26,18},{... | collective-permute-start | bytes 442376 | tf_op jit(solution)/shard_map/ppermute | solution.py:20
  112.7 5.6 collective-permute-start.10
  119.0 6.1 %collective-permute-start.11 = (f32[16,16,1,128]{3,2,1,0:T(1,128)S(1)}, f32[16,16,1,128]{3,2,1,0:T(1,128)S(1)}, u32[]{:S(2)}, u32[]{:S(2)}) collective-permute-start(f32[16,16,1,128]{3,2,1,0:T(1,128)S(1)} %get-tuple-element.74), channel_id=1, source_target_pairs={{1,0},{2,1},{3,2},{4,3},{5,4},{6,5},{7,6},{9,8},{10,9},{11,10},{12... | collective-permute-start | bytes 393224 | tf_op jit(solution)/shard_map/ppermute | solution.py:20
  133.8 7.2 %collective-permute-start.12 = (f32[1,16,2,8,128]{4,1,0,3,2:T(8,128)S(1)}, f32[1,16,2,8,128]{4,1,0,3,2:T(8,128)S(1)}, u32[]{:S(2)}, u32[]{:S(2)}) collective-permute-start(f32[1,16,2,8,128]{4,1,0,3,2:T(8,128)S(1)} %get-tuple-element.40), channel_id=1, source_target_pairs={{0,32},{32,64},{64,96},{96,128},{128,160},{160,192},{192,224},{1,3... | collective-permute-start | bytes 393224 | tf_op jit(solution)/shard_map/ppermute | solution.py:18
  138.4 6.7 %collective-permute-start.13 = (f32[1,16,2,8,128]{4,1,0,3,2:T(8,128)S(1)}, f32[1,16,2,8,128]{4,1,0,3,2:T(8,128)S(1)}, u32[]{:S(2)}, u32[]{:S(2)}) collective-permute-start(f32[1,16,2,8,128]{4,1,0,3,2:T(8,128)S(1)} %get-tuple-element.41), channel_id=1, source_target_pairs={{32,0},{64,32},{96,64},{128,96},{160,128},{192,160},{224,192},{33,... | collective-permute-start | bytes 393224 | tf_op jit(solution)/shard_map/ppermute | solution.py:20
  145.3 7.1 %collective-permute-start.14 = (f32[18,1,2,8,128]{4,1,0,3,2:T(1,128)S(1)}, f32[18,1,2,8,128]{4,1,0,3,2:T(1,128)S(1)}, u32[]{:S(2)}, u32[]{:S(2)}) collective-permute-start(f32[18,1,2,8,128]{4,1,0,3,2:T(1,128)S(1)} %get-tuple-element.24), channel_id=1, source_target_pairs={{0,8},{8,16},{16,24},{1,9},{9,17},{17,25},{2,10},{10,18},{18,26},{... | collective-permute-start | bytes 442376 | tf_op jit(solution)/shard_map/ppermute | solution.py:18
  149.5 6.5 %collective-permute-start.15 = (f32[18,1,2,8,128]{4,1,0,3,2:T(1,128)S(1)}, f32[18,1,2,8,128]{4,1,0,3,2:T(1,128)S(1)}, u32[]{:S(2)}, u32[]{:S(2)}) collective-permute-start(f32[18,1,2,8,128]{4,1,0,3,2:T(1,128)S(1)} %get-tuple-element.25), channel_id=1, source_target_pairs={{8,0},{16,8},{24,16},{9,1},{17,9},{25,17},{10,2},{18,10},{26,18},{... | collective-permute-start | bytes 442376 | tf_op jit(solution)/shard_map/ppermute | solution.py:20
  157.7 7.6 %collective-permute-start.16 = (f32[16,16,1,128]{3,1,0,2:T(8,128)S(1)}, f32[16,16,1,128]{3,1,0,2:T(8,128)S(1)}, u32[]{:S(2)}, u32[]{:S(2)}) collective-permute-start(f32[16,16,1,128]{3,1,0,2:T(8,128)S(1)} %dynamic-slice_bitcast_fusion.1), channel_id=1, source_target_pairs={{0,1},{1,2},{2,3},{3,4},{4,5},{5,6},{6,7},{8,9},{9,10},{10,11},{11... | collective-permute-start | bytes 393224 | tf_op jit(solution)/shard_map/ppermute | solution.py:18
  165.5 6.4 %collective-permute-start.17 = (f32[16,16,1,128]{3,1,0,2:T(8,128)S(1)}, f32[16,16,1,128]{3,1,0,2:T(8,128)S(1)}, u32[]{:S(2)}, u32[]{:S(2)}) collective-permute-start(f32[16,16,1,128]{3,1,0,2:T(8,128)S(1)} %get-tuple-element.70), channel_id=1, source_target_pairs={{1,0},{2,1},{3,2},{4,3},{5,4},{6,5},{7,6},{9,8},{10,9},{11,10},{12... | collective-permute-start | bytes 393224 | tf_op jit(solution)/shard_map/ppermute | solution.py:20
  192.4 6.6 %collective-permute-start.18 = (f32[1,16,2,8,128]{4,1,0,3,2:T(8,128)S(1)}, f32[1,16,2,8,128]{4,1,0,3,2:T(8,128)S(1)}, u32[]{:S(2)}, u32[]{:S(2)}) collective-permute-start(f32[1,16,2,8,128]{4,1,0,3,2:T(8,128)S(1)} %get-tuple-element.32), channel_id=1, source_target_pairs={{0,32},{32,64},{64,96},{96,128},{128,160},{160,192},{192,224},{1,3... | collective-permute-start | bytes 393224 | tf_op jit(solution)/shard_map/ppermute | solution.py:18
  196.1 6.4 %collective-permute-start.19 = (f32[1,16,2,8,128]{4,1,0,3,2:T(8,128)S(1)}, f32[1,16,2,8,128]{4,1,0,3,2:T(8,128)S(1)}, u32[]{:S(2)}, u32[]{:S(2)}) collective-permute-start(f32[1,16,2,8,128]{4,1,0,3,2:T(8,128)S(1)} %get-tuple-element.33), channel_id=1, source_target_pairs={{32,0},{64,32},{96,64},{128,96},{160,128},{192,160},{224,192},{33,... | collective-permute-start | bytes 393224 | tf_op jit(solution)/shard_map/ppermute | solution.py:20
  202.7 6.9 %collective-permute-start.20 = (f32[18,1,2,8,128]{4,1,0,3,2:T(1,128)S(1)}, f32[18,1,2,8,128]{4,1,0,3,2:T(1,128)S(1)}, u32[]{:S(2)}, u32[]{:S(2)}) collective-permute-start(f32[18,1,2,8,128]{4,1,0,3,2:T(1,128)S(1)} %get-tuple-element.22), channel_id=1, source_target_pairs={{0,8},{8,16},{16,24},{1,9},{9,17},{17,25},{2,10},{10,18},{18,26},{... | collective-permute-start | bytes 442376 | tf_op jit(solution)/shard_map/ppermute | solution.py:18
  206.9 6.5 %collective-permute-start.21 = (f32[18,1,2,8,128]{4,1,0,3,2:T(1,128)S(1)}, f32[18,1,2,8,128]{4,1,0,3,2:T(1,128)S(1)}, u32[]{:S(2)}, u32[]{:S(2)}) collective-permute-start(f32[18,1,2,8,128]{4,1,0,3,2:T(1,128)S(1)} %get-tuple-element.23), channel_id=1, source_target_pairs={{8,0},{16,8},{24,16},{9,1},{17,9},{25,17},{10,2},{18,10},{26,18},{... | collective-permute-start | bytes 442376 | tf_op jit(solution)/shard_map/ppermute | solution.py:20
  215.2 9.2 %collective-permute-start.22 = (f32[16,16,1,128]{3,1,0,2:T(8,128)S(1)}, f32[16,16,1,128]{3,1,0,2:T(8,128)S(1)}, u32[]{:S(2)}, u32[]{:S(2)}) collective-permute-start(f32[16,16,1,128]{3,1,0,2:T(8,128)S(1)} %dynamic-slice_bitcast_fusion), channel_id=1, source_target_pairs={{0,1},{1,2},{2,3},{3,4},{4,5},{5,6},{6,7},{8,9},{9,10},{10,11},{11... | collective-permute-start | bytes 393224 | tf_op jit(solution)/shard_map/ppermute | solution.py:18
  224.5 6.4 %collective-permute-start.23 = (f32[16,16,1,128]{3,1,0,2:T(8,128)S(1)}, f32[16,16,1,128]{3,1,0,2:T(8,128)S(1)}, u32[]{:S(2)}, u32[]{:S(2)}) collective-permute-start(f32[16,16,1,128]{3,1,0,2:T(8,128)S(1)} %get-tuple-element.68), channel_id=1, source_target_pairs={{1,0},{2,1},{3,2},{4,3},{5,4},{6,5},{7,6},{9,8},{10,9},{11,10},{12... | collective-permute-start | bytes 393224 | tf_op jit(solution)/shard_map/ppermute | solution.py:20
  232.2 11.2 %copy-start.22 = (bf16[2,7,2,8,2,8,128]{6,5,4,3,2,1,0:T(8,128)(2,1)}, bf16[2,7,2,8,2,8,128]{6,5,4,3,2,1,0:T(8,128)(2,1)S(1)}, u32[]{:S(2)}) copy-start(bf16[2,7,2,8,2,8,128]{6,5,4,3,2,1,0:T(8,128)(2,1)S(1)} %fusion.16) | copy-start | bytes 2752516
  330.6 3.4 copy-start.23
  336.7 4.4 copy-start.3
  (34 other events, 49.8 us)
Sparse Core Ops, SparseCore 0:
  336.8 251.9 all-reduce.46
where the time goes:
time: 610 us; the launch traced here: 601 us
  waiting for transfers between devices  300 us (49%)
  blocking collectives  84.3 us (14%)
  starting transfers between devices  71.9 us (12%)
  other arithmetic  53.6 us (9%)
  matrix products  43.4 us (7%)
  local copies, waits for them, and re-layouts  31.1 us (5%)
  between operations  17 us (3%)
    psum x1, waiting for transfers between devices, on_device(): stacked = lax.psum(stacked, ('gx', 'gy', 'gz'))  246 us
    psum x1, blocking collectives, on_device(): stacked = lax.psum(stacked, ('gx', 'gy', 'gz'))  84.3 us
    ppermute x12, starting transfers between devices, with_halo(): lax.ppermute(tail, axis, [(i, (i + 1) % count) for i in range(ends)])  53.2 us
    ppermute x12, waiting for transfers between devices, with_halo(): lax.ppermute(head, axis, [((i + 1) % count, i) for i in range(ends)])  46.7 us
    dot_general x31, matrix products, matmul_rows(): product = jnp.dot(flattened, weight, preferred_element_type=jnp.float32)  31.6 us
    ppermute x12, starting transfers between devices, with_halo(): lax.ppermute(head, axis, [((i + 1) % count, i) for i in range(ends)])  18.6 us
    unnamed x82, local copies, waits for them, and re-layouts  12.7 us
  transfers between devices with their start and end apart: 25, of which 21 were waited for; matrix products, arithmetic and copies ran while one was open for 3% of the time, Pallas kernels for 0%

commit v1 on v0

--- a/solution.py
+++ b/solution.py
@@ -3,6 +3,7 @@
 import jax.numpy as jnp
 from jax import lax
 from jax.sharding import PartitionSpec as P
+from jax.lax import psum
 
 edge_dims = (1, 3, 5)
 
@@ -251,7 +252,7 @@
     stacked = tuple(
         (jnp.stack([per_layer[0][pos_no], per_layer[1][pos_no]]) for pos_no in range(4))
     )
-    stacked = lax.psum(stacked, ("gx", "gy", "gz"))
+    stacked = psum(psum(stacked, "gx"), axis_name=("gy", "gz"))
     layers_all = 3 * slot_count * size_z // 4
     nodes_all = (
         nodes_edge**3 * elems_x * lax.axis_size("gx") * elems_y * lax.axis_size("gy") * layers_all

time: 610 us -> 554 us (0.908)
  waiting for transfers between devices: 300 us -> 239 us
  blocking collectives: 84.3 us -> 94 us
  matrix products: 43.4 us -> 36.1 us
    psum x1 -> x2, waiting for transfers between devices: 246 us -> 185 us  [on_device(): stacked = psum(psum(stacked, 'gx'), axis_name=('gy', 'gz'))]
    psum x1 -> x2, blocking collectives: 84.3 us -> 94 us  [on_device(): stacked = psum(psum(stacked, 'gx'), axis_name=('gy', 'gz'))]
    unnamed x82 -> x78, local copies, waits for them, and re-layouts: 12.7 us -> 13.7 us
  transfers between devices with their start and end apart: 25 -> 26, of which waited for: 21 -> 22; matrix products, arithmetic and copies ran while one was open for 3% -> 4% of each run, Pallas kernels for 0% -> 0%
where the time goes in v1:
time: 554 us; the launch traced here: 545 us
  waiting for transfers between devices  239 us (43%)
  blocking collectives  94 us (17%)
  starting transfers between devices  71.9 us (13%)
  other arithmetic  55.5 us (10%)
  matrix products  36.1 us (7%)
  local copies, waits for them, and re-layouts  32.1 us (6%)
  between operations  17 us (3%)
    psum x2, waiting for transfers between devices, on_device(): stacked = psum(psum(stacked, 'gx'), axis_name=('gy', 'gz'))  185 us
    psum x2, blocking collectives, on_device(): stacked = psum(psum(stacked, 'gx'), axis_name=('gy', 'gz'))  94 us
    ppermute x12, starting transfers between devices, with_halo(): lax.ppermute(tail, axis, [(i, (i + 1) % count) for i in range(ends)])  53.2 us
    ppermute x12, waiting for transfers between devices, with_halo(): lax.ppermute(head, axis, [((i + 1) % count, i) for i in range(ends)])  46.7 us
    dot_general x31, matrix products, matmul_rows(): product = jnp.dot(flattened, weight, preferred_element_type=jnp.float32)  27.2 us
    ppermute x12, starting transfers between devices, with_halo(): lax.ppermute(head, axis, [((i + 1) % count, i) for i in range(ends)])  18.6 us
    unnamed x78, local copies, waits for them, and re-layouts  13.7 us
  transfers between devices with their start and end apart: 26, of which 22 were waited for; matrix products, arithmetic and copies ran while one was open for 4% of the time, Pallas kernels for 0%

profile of v1, /device:TPU:1, one launch (start us, length us, event | category | flops | bytes accessed | tf_op | source)
XLA Modules:
  0.0 545.1 jit_solution(2615638030302375779)
XLA Ops:
  28.5 4.4 collective-permute-start
  34.3 2.4 copy_bitcast_fusion.7
  36.7 2.9 collective-permute-done.1
  41.3 4.7 collective-permute-start.2
  46.1 2.1 collective-permute-start.3
  48.5 4.4 collective-permute-done.3
  57.5 3.1 collective-permute-start.4
  64.3 4.5 collective-permute-done.5
  87.4 3.5 collective-permute-start.6
  93.5 5.2 collective-permute-done.7
  99.0 4.2 collective-permute-start.8
  105.3 4.4 collective-permute-done.9
  111.5 3.6 collective-permute-start.10
  120.4 3.5 collective-permute-done.11
  132.5 4.6 collective-permute-start.12
  139.7 4.1 collective-permute-done.13
  144.0 4.2 collective-permute-start.14
  151.2 3.6 collective-permute-done.15
  156.5 5.7 %collective-permute-start.16 = (f32[16,16,1,128]{3,1,0,2:T(8,128)S(1)}, f32[16,16,1,128]{3,1,0,2:T(8,128)S(1)}, u32[]{:S(2)}, u32[]{:S(2)}) collective-permute-start(f32[16,16,1,128]{3,1,0,2:T(8,128)S(1)} %dynamic-slice_bitcast_fusion.1), channel_id=1, source_target_pairs={{0,1},{1,2},{2,3},{3,4},{4,5},{5,6},{6,7},{8,9},{9,10},{10,11},{11... | collective-permute-start | bytes 393224 | tf_op jit(solution)/shard_map/ppermute | solution.py:19
  167.2 3.4 collective-permute-done.17
  189.5 3.6 collective-permute-start.18
  196.0 3.5 collective-permute-done.19
  199.7 4.2 collective-permute-start.20
  206.6 3.8 collective-permute-done.21
  212.3 7.2 %collective-permute-start.22 = (f32[16,16,1,128]{3,1,0,2:T(8,128)S(1)}, f32[16,16,1,128]{3,1,0,2:T(8,128)S(1)}, u32[]{:S(2)}, u32[]{:S(2)}) collective-permute-start(f32[16,16,1,128]{3,1,0,2:T(8,128)S(1)} %dynamic-slice_bitcast_fusion), channel_id=1, source_target_pairs={{0,1},{1,2},{2,3},{3,4},{4,5},{5,6},{6,7},{8,9},{9,10},{10,11},{11... | collective-permute-start | bytes 393224 | tf_op jit(solution)/shard_map/ppermute | solution.py:19
  224.6 3.4 collective-permute-done.23
  240.9 11.9 %psum.62 = f32[2,2,128]{2,1,0:T(2,128)S(1)} all-reduce(f32[2,2,128]{2,1,0:T(2,128)S(1)} %pad_maximum_fusion.51), channel_id=1, replica_groups=mesh['gx'=8,'gy'=4,'gz'=8] {'gx'}, use_global_device_ids=true, to_apply=%region_14.15 | all-reduce | flops 512 | bytes 4096 | tf_op jit(solution)/shard_map/psum | solution.py:255
  252.8 82.1 %psum.63 = f32[2,2,128]{2,1,0:T(2,128)S(1)} all-reduce(f32[2,2,128]{2,1,0:T(2,128)S(1)} %psum.62), channel_id=1, replica_groups=mesh['gx'=8,'gy'=4,'gz'=8] {'gy','gz'}, use_global_device_ids=true, to_apply=%region_15.16 | all-reduce | flops 512 | bytes 4096 | tf_op jit(solution)/shard_map/psum | solution.py:255
  339.7 4.4 subtract_add_fusion
  344.7 67.7 %all-reduce.51.cloned.1.call-done = (f32[2,2,128,128]{3,2,1,0:T(8,128)}, f32[2,256,128]{2,1,0:T(8,128)}, f32[2,128,128]{2,1,0:T(8,128)}) async-done(((f32[2,2,128,128]{3,2,1,0:T(8,128)}, f32[2,256,128]{2,1,0:T(8,128)}, f32[2,128,128]{2,1,0:T(8,128)}), (f32[2,2,128,128]{3,2,1,0:T(8,128)}, f32[2,256,128]{2,1,0:T(8,128)}, f32[2,128,128]{2,1,0:T(8,128)})) %all-reduce.51.cloned.1.call-update) | async-done | bytes 655376 | tf_op jit(solution)/shard_map/psum | solution.py:255
  412.5 3.0 fusion.43
  415.5 117.4 %all-reduce.49.cloned.1.call-done = (f32[2,2,128,128]{3,2,1,0:T(8,128)}, f32[2,256,128]{2,1,0:T(8,128)}, f32[2,128,128]{2,1,0:T(8,128)}) async-done(((f32[2,2,128,128]{3,2,1,0:T(8,128)}, f32[2,256,128]{2,1,0:T(8,128)}, f32[2,128,128]{2,1,0:T(8,128)}), (f32[2,2,128,128]{3,2,1,0:T(8,128)}, f32[2,256,128]{2,1,0:T(8,128)}, f32[2,128,128]{2,1,0:T(8,128)})) %all-reduce.49.cloned.1.call-update) | async-done | bytes 655376 | tf_op jit(solution)/shard_map/psum | solution.py:255
  (332 shorter events, 137.2 us)
Async XLA Ops:
  7.2 405.3 %all-reduce.51.cloned.1.call-start = ((), (), s32[]{:S(2)}) async-start(), calls=%async_computation.1 | async-start | bytes 1310720 | tf_op jit(solution)/shard_map/psum | solution.py:255
  8.9 6.6 %copy-start.15 = (bf16[2,7,2,8,2,8,128]{6,5,4,3,2,1,0:T(8,128)(2,1)}, bf16[2,7,2,8,2,8,128]{6,5,4,3,2,1,0:T(8,128)(2,1)S(1)}, u32[]{:S(2)}) copy-start(bf16[2,7,2,8,2,8,128]{6,5,4,3,2,1,0:T(8,128)(2,1)S(1)} %fusion.22) | copy-start | bytes 2752516
  12.3 7.7 %copy-start.30 = (f32[128]{0:T(128)}, f32[128]{0:T(128)S(1)}, u32[]{:S(2)}) copy-start(f32[128]{0:T(128)S(1)} %get-tuple-element.83) | copy-start | bytes 1540
  28.5 8.1 %collective-permute-start = (f32[1,16,2,8,128]{4,1,0,3,2:T(8,128)}, f32[1,16,2,8,128]{4,1,0,3,2:T(8,128)S(1)}, u32[]{:S(2)}, u32[]{:S(2)}) collective-permute-start(f32[1,16,2,8,128]{4,1,0,3,2:T(8,128)} %get-tuple-element.59), channel_id=1, source_target_pairs={{0,32},{32,64},{64,96},{96,128},{128,160},{160,192},{192,224},{1,3... | collective-permute-start | bytes 393224 | tf_op jit(solution)/shard_map/ppermute | solution.py:19
  32.9 6.7 %collective-permute-start.1 = (f32[1,16,2,8,128]{4,1,0,3,2:T(8,128)}, f32[1,16,2,8,128]{4,1,0,3,2:T(8,128)}, u32[]{:S(2)}, u32[]{:S(2)}) collective-permute-start(f32[1,16,2,8,128]{4,1,0,3,2:T(8,128)} %get-tuple-element.60), channel_id=1, source_target_pairs={{32,0},{64,32},{96,64},{128,96},{160,128},{192,160},{224,192},{33,... | collective-permute-start | bytes 393224 | tf_op jit(solution)/shard_map/ppermute | solution.py:21
  41.3 7.1 %collective-permute-start.2 = (f32[18,1,2,8,128]{4,1,0,3,2:T(1,128)}, f32[18,1,2,8,128]{4,1,0,3,2:T(1,128)S(1)}, u32[]{:S(2)}, u32[]{:S(2)}) collective-permute-start(f32[18,1,2,8,128]{4,1,0,3,2:T(1,128)} %get-tuple-element.33), channel_id=1, source_target_pairs={{0,8},{8,16},{16,24},{1,9},{9,17},{17,25},{2,10},{10,18},{18,26},{... | collective-permute-start | bytes 442376 | tf_op jit(solution)/shard_map/ppermute | solution.py:19
  46.1 6.8 %collective-permute-start.3 = (f32[18,1,2,8,128]{4,1,0,3,2:T(1,128)}, f32[18,1,2,8,128]{4,1,0,3,2:T(1,128)}, u32[]{:S(2)}, u32[]{:S(2)}) collective-permute-start(f32[18,1,2,8,128]{4,1,0,3,2:T(1,128)} %get-tuple-element.34), channel_id=1, source_target_pairs={{8,0},{16,8},{24,16},{9,1},{17,9},{25,17},{10,2},{18,10},{26,18},{... | collective-permute-start | bytes 442376 | tf_op jit(solution)/shard_map/ppermute | solution.py:21
  57.5 5.1 collective-permute-start.4
  62.6 6.1 %collective-permute-start.5 = (f32[16,16,1,128]{3,1,0,2:T(8,128)S(1)}, f32[16,16,1,128]{3,1,0,2:T(8,128)S(1)}, u32[]{:S(2)}, u32[]{:S(2)}) collective-permute-start(f32[16,16,1,128]{3,1,0,2:T(8,128)S(1)} %get-tuple-element.79), channel_id=1, source_target_pairs={{1,0},{2,1},{3,2},{4,3},{5,4},{6,5},{7,6},{9,8},{10,9},{11,10},{12... | collective-permute-start | bytes 393224 | tf_op jit(solution)/shard_map/ppermute | solution.py:21
  87.4 6.2 %collective-permute-start.6 = (f32[1,16,2,8,128]{4,1,0,2,3:T(8,128)S(1)}, f32[1,16,2,8,128]{4,1,0,2,3:T(8,128)S(1)}, u32[]{:S(2)}, u32[]{:S(2)}) collective-permute-start(f32[1,16,2,8,128]{4,1,0,2,3:T(8,128)S(1)} %get-tuple-element.51), channel_id=1, source_target_pairs={{0,32},{32,64},{64,96},{96,128},{128,160},{160,192},{192,224},{1,3... | collective-permute-start | bytes 393224 | tf_op jit(solution)/shard_map/ppermute | solution.py:19
  90.9 7.8 %collective-permute-start.7 = (f32[1,16,2,8,128]{4,1,0,2,3:T(8,128)S(1)}, f32[1,16,2,8,128]{4,1,0,2,3:T(8,128)S(1)}, u32[]{:S(2)}, u32[]{:S(2)}) collective-permute-start(f32[1,16,2,8,128]{4,1,0,2,3:T(8,128)S(1)} %get-tuple-element.52), channel_id=1, source_target_pairs={{32,0},{64,32},{96,64},{128,96},{160,128},{192,160},{224,192},{33,... | collective-permute-start | bytes 393224 | tf_op jit(solution)/shard_map/ppermute | solution.py:21
  99.0 6.3 %collective-permute-start.8 = (f32[18,1,2,8,128]{4,1,0,2,3:T(1,128)S(1)}, f32[18,1,2,8,128]{4,1,0,2,3:T(1,128)S(1)}, u32[]{:S(2)}, u32[]{:S(2)}) collective-permute-start(f32[18,1,2,8,128]{4,1,0,2,3:T(1,128)S(1)} %get-tuple-element.31), channel_id=1, source_target_pairs={{0,8},{8,16},{16,24},{1,9},{9,17},{17,25},{2,10},{10,18},{18,26},{... | collective-permute-start | bytes 442376 | tf_op jit(solution)/shard_map/ppermute | solution.py:19
  103.2 6.5 %collective-permute-start.9 = (f32[18,1,2,8,128]{4,1,0,2,3:T(1,128)S(1)}, f32[18,1,2,8,128]{4,1,0,2,3:T(1,128)S(1)}, u32[]{:S(2)}, u32[]{:S(2)}) collective-permute-start(f32[18,1,2,8,128]{4,1,0,2,3:T(1,128)S(1)} %get-tuple-element.32), channel_id=1, source_target_pairs={{8,0},{16,8},{24,16},{9,1},{17,9},{25,17},{10,2},{18,10},{26,18},{... | collective-permute-start | bytes 442376 | tf_op jit(solution)/shard_map/ppermute | solution.py:21
  111.5 5.6 %collective-permute-start.10 = (f32[16,16,1,128]{3,1,0,2:T(8,128)S(1)}, f32[16,16,1,128]{3,1,0,2:T(8,128)S(1)}, u32[]{:S(2)}, u32[]{:S(2)}) collective-permute-start(f32[16,16,1,128]{3,1,0,2:T(8,128)S(1)} %dynamic-slice_bitcast_fusion.2), channel_id=1, source_target_pairs={{0,1},{1,2},{2,3},{3,4},{4,5},{5,6},{6,7},{8,9},{9,10},{10,11},{11... | collective-permute-start | bytes 393224 | tf_op jit(solution)/shard_map/ppermute | solution.py:19
  117.8 6.1 %collective-permute-start.11 = (f32[16,16,1,128]{3,2,1,0:T(1,128)S(1)}, f32[16,16,1,128]{3,2,1,0:T(1,128)S(1)}, u32[]{:S(2)}, u32[]{:S(2)}) collective-permute-start(f32[16,16,1,128]{3,2,1,0:T(1,128)S(1)} %get-tuple-element.77), channel_id=1, source_target_pairs={{1,0},{2,1},{3,2},{4,3},{5,4},{6,5},{7,6},{9,8},{10,9},{11,10},{12... | collective-permute-start | bytes 393224 | tf_op jit(solution)/shard_map/ppermute | solution.py:21
  132.5 7.2 %collective-permute-start.12 = (f32[1,16,2,8,128]{4,1,0,3,2:T(8,128)S(1)}, f32[1,16,2,8,128]{4,1,0,3,2:T(8,128)S(1)}, u32[]{:S(2)}, u32[]{:S(2)}) collective-permute-start(f32[1,16,2,8,128]{4,1,0,3,2:T(8,128)S(1)} %get-tuple-element.43), channel_id=1, source_target_pairs={{0,32},{32,64},{64,96},{96,128},{128,160},{160,192},{192,224},{1,3... | collective-permute-start | bytes 393224 | tf_op jit(solution)/shard_map/ppermute | solution.py:19
  137.1 6.7 %collective-permute-start.13 = (f32[1,16,2,8,128]{4,1,0,3,2:T(8,128)S(1)}, f32[1,16,2,8,128]{4,1,0,3,2:T(8,128)S(1)}, u32[]{:S(2)}, u32[]{:S(2)}) collective-permute-start(f32[1,16,2,8,128]{4,1,0,3,2:T(8,128)S(1)} %get-tuple-element.44), channel_id=1, source_target_pairs={{32,0},{64,32},{96,64},{128,96},{160,128},{192,160},{224,192},{33,... | collective-permute-start | bytes 393224 | tf_op jit(solution)/shard_map/ppermute | solution.py:21
  144.0 7.1 %collective-permute-start.14 = (f32[18,1,2,8,128]{4,1,0,3,2:T(1,128)S(1)}, f32[18,1,2,8,128]{4,1,0,3,2:T(1,128)S(1)}, u32[]{:S(2)}, u32[]{:S(2)}) collective-permute-start(f32[18,1,2,8,128]{4,1,0,3,2:T(1,128)S(1)} %get-tuple-element.27), channel_id=1, source_target_pairs={{0,8},{8,16},{16,24},{1,9},{9,17},{17,25},{2,10},{10,18},{18,26},{... | collective-permute-start | bytes 442376 | tf_op jit(solution)/shard_map/ppermute | solution.py:19
  148.3 6.5 %collective-permute-start.15 = (f32[18,1,2,8,128]{4,1,0,3,2:T(1,128)S(1)}, f32[18,1,2,8,128]{4,1,0,3,2:T(1,128)S(1)}, u32[]{:S(2)}, u32[]{:S(2)}) collective-permute-start(f32[18,1,2,8,128]{4,1,0,3,2:T(1,128)S(1)} %get-tuple-element.28), channel_id=1, source_target_pairs={{8,0},{16,8},{24,16},{9,1},{17,9},{25,17},{10,2},{18,10},{26,18},{... | collective-permute-start | bytes 442376 | tf_op jit(solution)/shard_map/ppermute | solution.py:21
  156.5 7.6 %collective-permute-start.16 = (f32[16,16,1,128]{3,1,0,2:T(8,128)S(1)}, f32[16,16,1,128]{3,1,0,2:T(8,128)S(1)}, u32[]{:S(2)}, u32[]{:S(2)}) collective-permute-start(f32[16,16,1,128]{3,1,0,2:T(8,128)S(1)} %dynamic-slice_bitcast_fusion.1), channel_id=1, source_target_pairs={{0,1},{1,2},{2,3},{3,4},{4,5},{5,6},{6,7},{8,9},{9,10},{10,11},{11... | collective-permute-start | bytes 393224 | tf_op jit(solution)/shard_map/ppermute | solution.py:19
  164.2 6.4 %collective-permute-start.17 = (f32[16,16,1,128]{3,1,0,2:T(8,128)S(1)}, f32[16,16,1,128]{3,1,0,2:T(8,128)S(1)}, u32[]{:S(2)}, u32[]{:S(2)}) collective-permute-start(f32[16,16,1,128]{3,1,0,2:T(8,128)S(1)} %get-tuple-element.73), channel_id=1, source_target_pairs={{1,0},{2,1},{3,2},{4,3},{5,4},{6,5},{7,6},{9,8},{10,9},{11,10},{12... | collective-permute-start | bytes 393224 | tf_op jit(solution)/shard_map/ppermute | solution.py:21
  189.5 6.6 %collective-permute-start.18 = (f32[1,16,2,8,128]{4,1,0,3,2:T(8,128)S(1)}, f32[1,16,2,8,128]{4,1,0,3,2:T(8,128)S(1)}, u32[]{:S(2)}, u32[]{:S(2)}) collective-permute-start(f32[1,16,2,8,128]{4,1,0,3,2:T(8,128)S(1)} %get-tuple-element.35), channel_id=1, source_target_pairs={{0,32},{32,64},{64,96},{96,128},{128,160},{160,192},{192,224},{1,3... | collective-permute-start | bytes 393224 | tf_op jit(solution)/shard_map/ppermute | solution.py:19
  193.1 6.4 %collective-permute-start.19 = (f32[1,16,2,8,128]{4,1,0,3,2:T(8,128)S(1)}, f32[1,16,2,8,128]{4,1,0,3,2:T(8,128)S(1)}, u32[]{:S(2)}, u32[]{:S(2)}) collective-permute-start(f32[1,16,2,8,128]{4,1,0,3,2:T(8,128)S(1)} %get-tuple-element.36), channel_id=1, source_target_pairs={{32,0},{64,32},{96,64},{128,96},{160,128},{192,160},{224,192},{33,... | collective-permute-start | bytes 393224 | tf_op jit(solution)/shard_map/ppermute | solution.py:21
  199.7 6.9 %collective-permute-start.20 = (f32[18,1,2,8,128]{4,1,0,3,2:T(1,128)S(1)}, f32[18,1,2,8,128]{4,1,0,3,2:T(1,128)S(1)}, u32[]{:S(2)}, u32[]{:S(2)}) collective-permute-start(f32[18,1,2,8,128]{4,1,0,3,2:T(1,128)S(1)} %get-tuple-element.25), channel_id=1, source_target_pairs={{0,8},{8,16},{16,24},{1,9},{9,17},{17,25},{2,10},{10,18},{18,26},{... | collective-permute-start | bytes 442376 | tf_op jit(solution)/shard_map/ppermute | solution.py:19
  204.0 6.5 %collective-permute-start.21 = (f32[18,1,2,8,128]{4,1,0,3,2:T(1,128)S(1)}, f32[18,1,2,8,128]{4,1,0,3,2:T(1,128)S(1)}, u32[]{:S(2)}, u32[]{:S(2)}) collective-permute-start(f32[18,1,2,8,128]{4,1,0,3,2:T(1,128)S(1)} %get-tuple-element.26), channel_id=1, source_target_pairs={{8,0},{16,8},{24,16},{9,1},{17,9},{25,17},{10,2},{18,10},{26,18},{... | collective-permute-start | bytes 442376 | tf_op jit(solution)/shard_map/ppermute | solution.py:21
  212.3 9.2 %collective-permute-start.22 = (f32[16,16,1,128]{3,1,0,2:T(8,128)S(1)}, f32[16,16,1,128]{3,1,0,2:T(8,128)S(1)}, u32[]{:S(2)}, u32[]{:S(2)}) collective-permute-start(f32[16,16,1,128]{3,1,0,2:T(8,128)S(1)} %dynamic-slice_bitcast_fusion), channel_id=1, source_target_pairs={{0,1},{1,2},{2,3},{3,4},{4,5},{5,6},{6,7},{8,9},{9,10},{10,11},{11... | collective-permute-start | bytes 393224 | tf_op jit(solution)/shard_map/ppermute | solution.py:19
  221.6 6.4 %collective-permute-start.23 = (f32[16,16,1,128]{3,1,0,2:T(8,128)S(1)}, f32[16,16,1,128]{3,1,0,2:T(8,128)S(1)}, u32[]{:S(2)}, u32[]{:S(2)}) collective-permute-start(f32[16,16,1,128]{3,1,0,2:T(8,128)S(1)} %get-tuple-element.71), channel_id=1, source_target_pairs={{1,0},{2,1},{3,2},{4,3},{5,4},{6,5},{7,6},{9,8},{10,9},{11,10},{12... | collective-permute-start | bytes 393224 | tf_op jit(solution)/shard_map/ppermute | solution.py:21
  229.3 9.5 %copy-start.23 = (bf16[2,7,2,8,2,8,128]{6,5,4,3,2,1,0:T(8,128)(2,1)}, bf16[2,7,2,8,2,8,128]{6,5,4,3,2,1,0:T(8,128)(2,1)S(1)}, u32[]{:S(2)}) copy-start(bf16[2,7,2,8,2,8,128]{6,5,4,3,2,1,0:T(8,128)(2,1)S(1)} %fusion.16) | copy-start | bytes 2752516
  240.8 94.0 %copy-start.25 = (bf16[2,7,2,8,2,8,128]{6,5,4,3,2,1,0:T(8,128)(2,1)}, bf16[2,7,2,8,2,8,128]{6,5,4,3,2,1,0:T(8,128)(2,1)S(1)}, u32[]{:S(2)}) copy-start(bf16[2,7,2,8,2,8,128]{6,5,4,3,2,1,0:T(8,128)(2,1)S(1)} %get-tuple-element.112) | copy-start | bytes 2752516
  240.8 95.7 %copy-start.18 = (bf16[2,7,2,8,2,8,128]{6,5,4,3,2,1,0:T(8,128)(2,1)S(1)}, bf16[2,7,2,8,2,8,128]{6,5,4,3,2,1,0:T(8,128)(2,1)}, u32[]{:S(2)}) copy-start(bf16[2,7,2,8,2,8,128]{6,5,4,3,2,1,0:T(8,128)(2,1)} %copy-done.17) | copy-start | bytes 2752516
  339.2 193.6 %all-reduce.49.cloned.1.call-start = ((), (), s32[]{:S(2)}) async-start(), calls=%async_computation | async-start | bytes 1310720 | tf_op jit(solution)/shard_map/psum | solution.py:255
  339.7 72.8 %copy-start.4 = (bf16[16,16,2,8,128]{4,3,2,1,0:T(8,128)(2,1)S(1)}, bf16[16,16,2,8,128]{4,3,2,1,0:T(8,128)(2,1)}, u32[]{:S(2)}) copy-start(bf16[16,16,2,8,128]{4,3,2,1,0:T(8,128)(2,1)} %copy-done.3) | copy-start | bytes 3145732
  (33 other events, 50.1 us)
Sparse Core Ops, SparseCore 0:
  339.3 73.0 all-reduce.50
  416.0 116.8 all-reduce.48
